TPU v7x, 32 devices: a whole 2x2x4 slice. The times are simulated.
32 devices in a mesh: group: 4 (over z), dev: 8 (over y, x, core).
Axes of the slice: x: 2, y: 2, z: 4, core: 2. Of those that a mesh axis runs over, the one named last changes fastest.
Arguments:
- tile_values: bfloat16 [512, 128, 128], P(('group', 'dev')), may hold values from -0.25 to 0.25
- tile_rows: int32 [512], P(('group', 'dev')), may hold values from 0 to 1
- tile_columns: int32 [512], P(('group', 'dev')), may hold values from 0 to 15
- tile_count: int32 [32], P(('group', 'dev')), may hold values from 4 to 16, as said below
- start_basis: bfloat16 [8192, 64], P(('group', 'dev')), may hold values from -6 to 6
- seed_rows: int32 [1024], replicated, may hold values from 0 to 8191
Outputs:
- unit_embedding: float32 [8192, 64], P(('group', 'dev'))
- centroids: float32 [1024, 64], replicated
Inputs may be any that keep to these rules, and one draw needn't show every extreme that they name: `tile_count`: the most, 16, is reached by some device in every draw.
All inputs are finite; a program needn't handle non-finite values.
Results may differ from a plain program's by a relative error of at most 0.0029.
Values may be sent and summed in bfloat16 or wider, within the bound.
A program may use at most 64 MiB of HBM per device.

v0:
```python
import math

import jax
import jax.numpy as jnp
from jax import lax
from jax.sharding import PartitionSpec as P

ITERS = 2
KSTEPS = 2


sharpness = 4.0


def apply_tiles(
    tile_block, row_index, column_index, live_count, group_basis, row_blocks, slot_group
):
    block = tile_block.shape[1]
    width = group_basis.shape[1]
    basis_blocks = group_basis.reshape(-1, block, width)
    turns = (live_count + slot_group - 1) // slot_group
    block_index = jnp.arange(row_blocks, dtype=jnp.int32)

    def advance(turn_index, total):
        first = turn_index * slot_group
        values_part = lax.dynamic_slice_in_dim(tile_block, first, slot_group, 0)
        rows_part = lax.dynamic_slice_in_dim(row_index, first, slot_group, 0)
        columns_part = lax.dynamic_slice_in_dim(column_index, first, slot_group, 0)
        picked = jnp.take(basis_blocks, columns_part, axis=0)
        products = jnp.einsum(
            "tij,tjk->tik", values_part, picked, preferred_element_type=jnp.float32
        )
        live = first + jnp.arange(slot_group, dtype=jnp.int32) < live_count
        select = ((rows_part[None, :] == block_index[:, None]) & live[None, :]).astype(jnp.float32)
        return total + jnp.einsum("rt,tik->rik", select, products, precision=lax.Precision.HIGHEST)

    total = lax.fori_loop(0, turns, advance, jnp.zeros((row_blocks, block, width), jnp.float32))
    return total.reshape(row_blocks * block, width)


def local(tile_values, tile_rows, tile_columns, tile_count, start_basis, seed_rows):
    block = tile_values.shape[1]
    slots = tile_values.shape[0]
    local_rows = start_basis.shape[0]
    row_blocks = local_rows // block
    slot_group = math.gcd(8, slots)
    own_count = tile_count[0]
    total_rows = local_rows * lax.axis_size("group") * lax.axis_size("dev")
    basis = start_basis
    embedding = None
    for step_index in range(ITERS):
        group_basis = lax.all_gather(basis, "dev", axis=0, tiled=True)
        image = apply_tiles(
            tile_values, tile_rows, tile_columns, own_count, group_basis, row_blocks, slot_group
        )
        gram = lax.psum(jnp.dot(image.T, image, precision=lax.Precision.HIGHEST), ("group", "dev"))
        lower = jnp.linalg.cholesky(gram)
        solved = lax.linalg.triangular_solve(
            lower, image, left_side=False, lower=True, transpose_a=True
        )
        if step_index + 1 < ITERS:
            basis = solved.astype(jnp.bfloat16)
        else:
            embedding = solved * jnp.sqrt(jnp.float32(total_rows))
    unit = embedding / jnp.sqrt(jnp.sum(embedding * embedding, axis=1, keepdims=True) + 1e-06)
    first_row = (
        lax.axis_index("group") * lax.axis_size("dev") + lax.axis_index("dev")
    ) * local_rows
    chooser = (
        seed_rows[:, None] - first_row == jnp.arange(local_rows, dtype=jnp.int32)[None, :]
    ).astype(jnp.float32)
    centres = lax.psum(jnp.dot(chooser, unit, precision=lax.Precision.HIGHEST), ("group", "dev"))
    unit_square = jnp.sum(unit * unit, axis=1)
    for kstep in range(KSTEPS):
        dist = (
            unit_square[:, None]
            - 2.0 * jnp.dot(unit, centres.T, precision=lax.Precision.HIGHEST)
            + jnp.sum(centres * centres, axis=1)[None, :]
        )
        weights = jnp.exp(-sharpness * dist)
        member = weights / jnp.sum(weights, axis=1, keepdims=True)
        weighted = jnp.dot(member.T, unit, precision=lax.Precision.HIGHEST)
        mass = jnp.sum(member, axis=0)
        weighted, mass = lax.psum((weighted, mass), ("group", "dev"))
        centres = weighted / mass[:, None]
    return (unit, centres)


def solution(mesh):
    return jax.shard_map(
        local,
        mesh=mesh,
        in_specs=(
            P(("group", "dev"), None, None),
            P(("group", "dev")),
            P(("group", "dev")),
            P(("group", "dev")),
            P(("group", "dev"), None),
            P(),
        ),
        out_specs=(P(("group", "dev"), None), P()),
        check_vma=False,
    )
```

profile of v0, /device:TPU:0, one launch (start us, length us, event | category | flops | bytes accessed | tf_op | source)
XLA Modules:
  0.0 544.6 jit_solution(14155471311787401362)
XLA Ops:
  7.9 11.4 %all_gather.6 = bf16[2048,64]{0,1:T(8,128)(2,1)S(1)} all-gather(bf16[256,64]{0,1:T(8,128)(2,1)S(1)} %copy-done.5), channel_id=1, replica_groups=mesh['group'=4,'dev'=8] {'dev'}, dimensions={0}, use_global_device_ids=true | all-gather | bytes 294912 | tf_op jit(solution)/shard_map/all_gather | solution.py:52
  19.4 0.3 copy.8
  19.7 0.6 copy-done.4
  20.3 4.7 while.22
  20.4 0.7 compare_and_fusion.4
  21.1 0.6 gather_fusion
  21.8 0.4 fusion.84
  22.2 0.5 convolution_add_fusion.4
  22.8 0.7 compare_and_fusion.4
  23.5 0.6 gather_fusion
  24.1 0.4 fusion.84
  24.5 0.5 convolution_add_fusion.4
  25.2 39.2 %psum.49 = f32[64,64]{0,1:T(8,128)S(1)} all-reduce(f32[64,64]{0,1:T(8,128)S(1)} %convolution_bitcast_fusion.3), channel_id=1, replica_groups=mesh['group'=4,'dev'=8] {'group','dev'}, use_global_device_ids=true, to_apply=%region_2.4 | all-reduce | flops 4096 | bytes 32768 | tf_op jit(solution)/shard_map/psum | solution.py:56
  64.5 5.8 %cholesky.44 = f32[64,64]{1,0:T(8,128)S(1)} custom-call(f32[64,64]{1,0:T(8,128)S(1)} %fusion.59), custom_call_target="Cholesky" | custom-call | tf_op jit(solution)/shard_map/jit(cholesky)/cholesky | solution.py:57
  70.4 0.7 compare_reduce_fusion.1
  71.1 0.7 fusion.54
  71.8 4.9 custom-call.6
  77.0 10.6 %all_gather.7 = bf16[2048,64]{0,1:T(8,128)(2,1)S(1)} all-gather(bf16[256,64]{0,1:T(8,128)(2,1)S(1)} %fusion.41), channel_id=1, replica_groups=mesh['group'=4,'dev'=8] {'dev'}, dimensions={0}, use_global_device_ids=true | all-gather | bytes 294912 | tf_op jit(solution)/shard_map/all_gather | solution.py:52
  87.6 0.3 copy.23
  87.9 4.7 while.23
  88.0 0.7 compare_and_fusion.5
  88.8 0.6 gather_fusion.1
  89.4 0.4 fusion.89
  89.8 0.5 convolution_add_fusion.5
  90.4 0.7 compare_and_fusion.5
  91.1 0.6 gather_fusion.1
  91.7 0.4 fusion.89
  92.1 0.5 convolution_add_fusion.5
  92.9 38.5 %psum.50 = f32[64,64]{0,1:T(8,128)S(1)} all-reduce(f32[64,64]{0,1:T(8,128)S(1)} %convolution_bitcast_fusion.2), channel_id=1, replica_groups=mesh['group'=4,'dev'=8] {'group','dev'}, use_global_device_ids=true, to_apply=%region_7.11 | all-reduce | flops 4096 | bytes 32768 | tf_op jit(solution)/shard_map/psum | solution.py:56
  131.5 5.8 %cholesky.55 = f32[64,64]{1,0:T(8,128)S(1)} custom-call(f32[64,64]{1,0:T(8,128)S(1)} %fusion.57), custom_call_target="Cholesky" | custom-call | tf_op jit(solution)/shard_map/jit(cholesky)/cholesky | solution.py:57
  137.4 0.6 compare_reduce_fusion
  138.0 0.7 fusion.55
  138.7 4.9 custom-call.7
  143.6 0.3 multiply_reduce_fusion.3
  143.9 0.7 copy-done.6
  144.6 1.4 fusion.42
  146.1 126.6 %all-reduce.4.cloned.1.call-done = f32[1024,64]{0,1:T(8,128)} async-done(((f32[1024,64]{0,1:T(8,128)}), f32[1024,64]{0,1:T(8,128)}) %all-reduce.4.cloned.1.call-update) | async-done | bytes 262160 | tf_op jit(solution)/shard_map/psum | solution.py:72
  272.7 1.1 multiply_reduce_fusion.1
  273.7 1.3 fusion.62
  275.0 1.6 fusion.45
  276.9 39.5 %psum.53 = f32[1024]{0:T(1024)S(1)} all-reduce(f32[1024]{0:T(1024)S(1)} %fusion.44), channel_id=1, replica_groups=mesh['group'=4,'dev'=8] {'group','dev'}, use_global_device_ids=true, to_apply=%region_15.19 | all-reduce | flops 1024 | bytes 8192 | tf_op jit(solution)/shard_map/psum | solution.py:84
  316.4 88.1 %all-reduce.6.cloned.1.call-done = f32[1024,64]{0,1:T(8,128)} async-done(((f32[1024,64]{0,1:T(8,128)}), f32[1024,64]{0,1:T(8,128)}) %all-reduce.6.cloned.1.call-update) | async-done | bytes 262160 | tf_op jit(solution)/shard_map/psum | solution.py:84
  404.5 1.1 multiply_reduce_fusion
  405.6 1.3 fusion.63
  406.9 1.6 fusion.47
  408.7 39.4 %psum.55 = f32[1024]{0:T(1024)S(1)} all-reduce(f32[1024]{0:T(1024)S(1)} %fusion.46), channel_id=1, replica_groups=mesh['group'=4,'dev'=8] {'group','dev'}, use_global_device_ids=true, to_apply=%region_20.24 | all-reduce | flops 1024 | bytes 8192 | tf_op jit(solution)/shard_map/psum | solution.py:84
  448.1 88.3 %all-reduce.8.cloned.1.call-done = f32[1024,64]{0,1:T(8,128)} async-done(((f32[1024,64]{0,1:T(8,128)}), f32[1024,64]{0,1:T(8,128)}) %all-reduce.8.cloned.1.call-update) | async-done | bytes 262160 | tf_op jit(solution)/shard_map/psum | solution.py:84
  536.4 1.7 broadcast_divide_fusion.4
  (44 shorter events, 1.9 us)
Async XLA Ops:
  7.2 0.8 copy-start.5
  7.2 265.5 %all-reduce.4.cloned.1.call-start = ((), (), s32[]{:S(2)}) async-start(), calls=%async_computation | async-start | bytes 524288 | tf_op jit(solution)/shard_map/psum | solution.py:72
  7.9 11.8 %copy-start = (bf16[16,128,128]{2,1,0:T(8,128)(2,1)S(1)}, bf16[16,128,128]{2,1,0:T(8,128)(2,1)}, u32[]{:S(2)}) copy-start(bf16[16,128,128]{2,1,0:T(8,128)(2,1)} %param.15) | copy-start | bytes 1572868
  19.7 0.7 copy-start.4
  19.7 0.7 copy-start.7
  143.8 0.7 copy-start.6
  144.6 262.3 %copy-start.3 = (f32[256,64]{0,1:T(8,128)}, f32[256,64]{0,1:T(8,128)S(1)}, u32[]{:S(2)}) copy-start(f32[256,64]{0,1:T(8,128)S(1)} %get-tuple-element.186) | copy-start | bytes 196612
  146.0 258.5 %all-reduce.6.cloned.1.call-start = ((), (), s32[]{:S(2)}) async-start(), calls=%async_computation.1 | async-start | bytes 524288 | tf_op jit(solution)/shard_map/psum | solution.py:84
  272.7 1.1 copy-start.2
  276.7 259.7 %all-reduce.8.cloned.1.call-start = ((), (), s32[]{:S(2)}) async-start(), calls=%async_computation.2 | async-start | bytes 524288 | tf_op jit(solution)/shard_map/psum | solution.py:84
  404.5 1.1 copy-start.1
Sparse Core Ops, SparseCore 0:
  146.1 126.4 all-reduce.3
  278.8 125.7 all-reduce.5
  410.6 125.7 all-reduce.7
where the time goes:
time: 545 us
  waiting for transfers between devices  303 us (56%)
  blocking collectives  179 us (33%)
  other arithmetic  31.4 us (6%)
  between operations  14.6 us (3%)
  matrix products  11.8 us (2%)
    psum x2, waiting for transfers between devices, local(): weighted, mass = lax.psum((weighted, mass), ('group', 'dev'))  176 us
    psum x1, waiting for transfers between devices, local(): lax.psum(jnp.dot(chooser, unit, precision=lax.Precision.HIGHEST), ('group...  127 us
    psum x2, blocking collectives, local(): weighted, mass = lax.psum((weighted, mass), ('group', 'dev'))  78.9 us
    psum x2, blocking collectives, local(): lax.psum(jnp.dot(image.T, image, precision=lax.Precision.HIGHEST), ('grou...  77.7 us
    all_gather x2, blocking collectives, local(): group_basis = lax.all_gather(basis, 'dev', axis=0, tiled=True)  22.1 us
    another operation x6, other arithmetic, local(): lower = jnp.linalg.cholesky(gram)  13.1 us
    another operation x4, other arithmetic, local(): lax.linalg.triangular_solve(lower, image, left_side=False, lower=True, tr...  11.1 us
  transfers between devices with their start and end apart: 3, of which 3 were waited for; matrix products, arithmetic and copies ran while one was open for 0% of the time, Pallas kernels for 0%

commit v1 on v0

v1 whole, which is shorter than its diff:
```python
import functools

import jax
import jax.numpy as jnp
from jax import lax
from jax.experimental import pallas as pl
from jax.experimental.pallas import tpu as pltpu
from jax.sharding import PartitionSpec as P

KSTEPS = 2
SHARPNESS = 4.0
MESH = pl.DeviceIdType.MESH
F32 = jnp.float32
HIGHEST = lax.Precision.HIGHEST
NN = (((1,), (0,)), ((), ()))
NT = (((1,), (1,)), ((), ()))


def mm(a, b, dims=NN):
    return lax.dot_general(a, b, dims, precision=HIGHEST, preferred_element_type=F32)


def loop(n, body):
    if n <= 8:
        for i in range(n):
            body(i)
    else:

        def step(i, carry):
            body(i)
            return carry

        lax.fori_loop(0, n, step, 0)


def fold(n, ref):
    if n <= 8:
        total = ref[0]
        for i in range(1, n):
            total = total + ref[i]
        return total
    return lax.fori_loop(1, n, lambda i, total: total + ref[i], ref[0])


class Exchange:
    def __init__(self, axis, n, me, land, sems, source=None):
        self.axis, self.n, self.me = axis, n, me
        self.land, self.source = land, source
        self.send, self.recv = sems

    def copy(self, peer, slot):
        source = self.land(self.me) if self.source is None else self.source(peer)
        return pltpu.make_async_remote_copy(
            src_ref=source,
            dst_ref=self.land(slot),
            send_sem=self.send.at[peer],
            recv_sem=self.recv.at[slot],
            device_id={self.axis: peer},
            device_id_type=MESH,
        )

    def peer(self, i):
        return lax.rem(self.me + 1 + i, self.n)

    def start(self):
        loop(self.n - 1, lambda i: self.copy(self.peer(i), self.me).start())

    def wait_recv(self):
        loop(self.n - 1, lambda i: self.copy(self.peer(i), self.peer(i)).wait_recv())

    def wait_send(self):
        loop(self.n - 1, lambda i: self.copy(self.peer(i), self.me).wait_send())


def factor_inverse(gram):
    k = gram.shape[0]
    rows = lax.broadcasted_iota(jnp.int32, (k, k), 0)
    lanes = lax.broadcasted_iota(jnp.int32, (k, k), 1)
    table = jnp.concatenate([gram, jnp.where(rows == lanes, 1.0, 0.0).astype(F32)], axis=1)
    parts = [table[8 * b : 8 * b + 8] for b in range(k // 8)]
    sub = lax.broadcasted_iota(jnp.int32, (8, 2 * k), 0)
    for i in range(k):
        b, r = divmod(i, 8)
        row = parts[b][r : r + 1]
        scaled = row / row[:, i : i + 1]
        own = parts[b] - parts[b][:, i : i + 1] * scaled
        if r < 7:
            parts[b] = jnp.where(sub > r, own, parts[b])
        for c in range(b + 1, k // 8):
            parts[c] = parts[c] - parts[c][:, i : i + 1] * scaled
    table = jnp.concatenate(parts, axis=0)
    diag = jnp.sum(jnp.where(rows == lanes, table[:, :k], 0.0), axis=1, keepdims=True)
    return table[:, k:] / jnp.sqrt(diag)


def pack(gram):
    half = gram.shape[0] // 2
    return jnp.concatenate([gram[:half], gram[half:]], axis=1)


def unpack(packed):
    k = packed.shape[1] // 2
    return jnp.concatenate([packed[:, :k], packed[:, k:]], axis=0)


def kernel(
    n, m, total_rows,
    tiles, rows_ref, columns_ref, count_ref, start, seeds,
    unit_out, centres_out,
    matrix, basis0, basis1, images, gram_dev, gram_group,
    seed_out, seed_dev, seed_group, seed_all,
    k_out, k_dev, k_group, k_all,
    *sems,
):
    me, g = lax.axis_index("dev"), lax.axis_index("group")
    pairs = [(sems[2 * i], sems[2 * i + 1]) for i in range(len(sems) // 2)]
    slots, block = tiles.shape[0], tiles.shape[1]
    local_rows, width = start.shape
    row_blocks = local_rows // block
    clusters = seeds.shape[1]
    part = clusters // n

    barrier = pltpu.get_barrier_semaphore()
    for axis, size, index in (("dev", n, me), ("group", m, g)):
        loop(
            size - 1,
            lambda i: pl.semaphore_signal(
                barrier, inc=1, device_id={axis: lax.rem(index + 1 + i, size)}, device_id_type=MESH
            ),
        )
    eye = jnp.where(
        lax.broadcasted_iota(jnp.int32, (width, width), 0)
        == lax.broadcasted_iota(jnp.int32, (width, width), 1),
        1.0,
        0.0,
    ).astype(jnp.bfloat16)
    start_t = lax.dot_general(eye, start[...], NT, preferred_element_type=F32)
    for r in range(row_blocks):
        basis0[me * row_blocks + r] = start_t[:, r * block : (r + 1) * block].astype(jnp.bfloat16)
    pl.semaphore_wait(barrier, n - 1 + m - 1)

    used = iter(pairs)
    pending = []

    def exchange(axis, land, source=None):
        size, index = (n, me) if axis == "dev" else (m, g)
        made = Exchange(axis, size, index, land, next(used), source)
        made.start()
        pending.append(made)
        return made

    own_blocks = lambda d: basis0.at[pl.ds(d * row_blocks, row_blocks)]
    gather = exchange("dev", own_blocks)
    count = count_ref[0]
    for s in range(slots):
        for r in range(row_blocks):
            keep = jnp.logical_and(rows_ref[s] == r, s < count)
            matrix[r * block : (r + 1) * block, s * block : (s + 1) * block] = tiles[s] * jnp.where(
                keep, 1.0, 0.0
            ).astype(jnp.bfloat16)

    def apply(basis):
        picked = jnp.concatenate([basis[columns_ref[s]] for s in range(slots)], axis=1)
        return lax.dot_general(picked, matrix[...], NT, preferred_element_type=F32)

    def start_gram(image, turn):
        gram_dev[turn, me] = pack(mm(image, image, NT))
        return exchange("dev", lambda d: gram_dev.at[turn, d])

    def end_gram(first, turn):
        first.wait_recv()
        gram_group[turn, g] = fold(n, gram_dev.at[turn])
        return exchange("group", lambda d: gram_group.at[turn, d])

    gather.wait_recv()
    image = apply(basis0)
    first = start_gram(image, 0)
    images[me] = image
    gather = exchange("dev", lambda d: images.at[d])
    second = end_gram(first, 0)
    second.wait_recv()
    inverse = factor_inverse(unpack(fold(m, gram_group.at[0])))
    gather.wait_recv()

    def solve(d):
        solved = mm(inverse, images[d])
        for r in range(row_blocks):
            basis1[d * row_blocks + r] = solved[:, r * block : (r + 1) * block].astype(jnp.bfloat16)

    loop(n, solve)
    image = apply(basis1)
    first = start_gram(image, 1)

    def split(values, out, lo, hi):
        for c in range(n):
            out[c, lo:hi] = values[:, c * part : (c + 1) * part]

    def join(ref):
        return jnp.concatenate([ref[c] for c in range(n)], axis=1)

    first_row = (g * n + me) * local_rows
    chooser = jnp.where(
        lax.broadcasted_iota(jnp.int32, (local_rows, clusters), 0) == seeds[...] - first_row, 1.0, 0.0
    ).astype(F32)
    split(mm(image, chooser), seed_out, 0, width)
    seed_dev[me] = seed_out[me]
    reduce_dev = exchange("dev", lambda d: seed_dev.at[d], lambda p: seed_out.at[p])
    second = end_gram(first, 1)
    reduce_dev.wait_recv()
    seed_group[g] = fold(n, seed_dev)
    reduce_group = exchange("group", lambda d: seed_group.at[d])
    second.wait_recv()
    packed = fold(m, gram_group.at[1])
    reduce_group.wait_recv()
    seed_all[me] = fold(m, seed_group)
    gather = exchange("dev", lambda d: seed_all.at[d])
    inverse = factor_inverse(unpack(packed))

    def normalise(image_t):
        embedding = mm(inverse, image_t) * jnp.sqrt(F32(total_rows))
        return embedding / jnp.sqrt(jnp.sum(embedding * embedding, axis=0, keepdims=True) + 1e-06)

    unit_t = normalise(image)
    unit = unit_t.T
    unit_out[...] = unit
    unit_square = jnp.sum(unit * unit, axis=1, keepdims=True)
    gather.wait_recv()
    centres = normalise(join(seed_all))
    for turn in range(KSTEPS):
        dist = unit_square - 2.0 * mm(unit, centres) + jnp.sum(centres * centres, axis=0, keepdims=True)
        weights = jnp.exp(-SHARPNESS * dist)
        member = weights / jnp.sum(weights, axis=1, keepdims=True)
        split(mm(unit_t, member), k_out.at[turn], 0, width)
        mass = jnp.sum(member, axis=0, keepdims=True)
        split(jnp.broadcast_to(mass, (8, clusters)), k_out.at[turn], width, width + 8)
        k_dev[turn, me] = k_out[turn, me]
        reduce_dev = exchange(
            "dev", lambda d: k_dev.at[turn, d], lambda p: k_out.at[turn, p]
        )
        reduce_dev.wait_recv()
        k_group[turn, g] = fold(n, k_dev.at[turn])
        reduce_group = exchange("group", lambda d: k_group.at[turn, d])
        reduce_group.wait_recv()
        sums = fold(m, k_group.at[turn])
        k_all[turn, me] = sums[:width] / sums[width : width + 1]
        gather = exchange("dev", lambda d: k_all.at[turn, d])
        gather.wait_recv()
        centres = join(k_all.at[turn])
    centres_out[...] = centres.T
    for made in pending:
        made.wait_send()


def local(tile_values, tile_rows, tile_columns, tile_count, start_basis, seed_rows):
    n, m = lax.axis_size("dev"), lax.axis_size("group")
    slots, block = tile_values.shape[0], tile_values.shape[1]
    local_rows, width = start_basis.shape
    row_blocks = local_rows // block
    clusters = seed_rows.shape[0]
    part = clusters // n
    vmem = pl.BlockSpec(memory_space=pltpu.VMEM)
    smem = pl.BlockSpec(memory_space=pltpu.SMEM)
    half = (width // 2, 2 * width)
    axes = ["dev", "dev", "dev", "group", "dev", "dev", "group", "group", "dev"]
    axes += ["dev", "group", "dev"] * KSTEPS
    sems = []
    for axis in axes:
        sems += [pltpu.SemaphoreType.DMA((n if axis == "dev" else m,))] * 2
    return pl.pallas_call(
        functools.partial(kernel, n, m, local_rows * n * m),
        out_shape=(
            jax.ShapeDtypeStruct((local_rows, width), F32),
            jax.ShapeDtypeStruct((clusters, width), F32),
        ),
        in_specs=[vmem, smem, smem, smem, vmem, vmem],
        out_specs=(vmem, vmem),
        scratch_shapes=[
            pltpu.VMEM((local_rows, slots * block), jnp.bfloat16),
            pltpu.VMEM((n * row_blocks, width, block), jnp.bfloat16),
            pltpu.VMEM((n * row_blocks, width, block), jnp.bfloat16),
            pltpu.VMEM((n, width, local_rows), F32),
            pltpu.VMEM((2, n, *half), F32),
            pltpu.VMEM((2, m, *half), F32),
            pltpu.VMEM((n, width, part), F32),
            pltpu.VMEM((n, width, part), F32),
            pltpu.VMEM((m, width, part), F32),
            pltpu.VMEM((n, width, part), F32),
            pltpu.VMEM((KSTEPS, n, width + 8, part), F32),
            pltpu.VMEM((KSTEPS, n, width + 8, part), F32),
            pltpu.VMEM((KSTEPS, m, width + 8, part), F32),
            pltpu.VMEM((KSTEPS, n, width, part), F32),
            *sems,
        ],
        compiler_params=pltpu.CompilerParams(
            collective_id=0, has_side_effects=True, vmem_limit_bytes=58 * 1024 * 1024
        ),
        name="spectral",
    )(tile_values, tile_rows, tile_columns, tile_count, start_basis, seed_rows[None, :])


def solution(mesh):
    return jax.shard_map(
        local,
        mesh=mesh,
        in_specs=(
            P(("group", "dev"), None, None),
            P(("group", "dev")),
            P(("group", "dev")),
            P(("group", "dev")),
            P(("group", "dev"), None),
            P(),
        ),
        out_specs=(P(("group", "dev"), None), P()),
        check_vma=False,
    )
```

time: 545 us -> 90 us (0.17)
  waiting for transfers between devices: 303 us -> 0 us
  blocking collectives: 179 us -> 0 us
  Pallas kernels: 0 us -> 83.4 us
  other arithmetic: 31.4 us -> 0 us
  between operations: 14.6 us -> 1.29 us
  matrix products: 11.8 us -> 0 us
    psum x3 -> x0, waiting for transfers between devices: 303 us -> none  [the longest x2 176 us: local(): weighted, mass = lax.psum((weighted, mass), ('group', 'dev'))]
    psum x4 -> x0, blocking collectives: 157 us -> none  [the longest x2 78.9 us: local(): weighted, mass = lax.psum((weighted, mass), ('group', 'dev'))]
    pallas_call x0 -> x1, Pallas kernels: none -> 83.4 us  [local(): pl.pallas_call(functools.partial(kernel, n, m, local_rows * n * m), out_s...]
    another operation x10 -> x0, other arithmetic: 24.3 us -> none  [the longest x6 13.1 us: local(): lower = jnp.linalg.cholesky(gram)]
    all_gather x2 -> x0, blocking collectives: 22.1 us -> none  [local(): group_basis = lax.all_gather(basis, 'dev', axis=0, tiled=True)]
    dot_general x15 -> x0, matrix products: 11.3 us -> none  [the longest x2 3.23 us: local(): weighted = jnp.dot(member.T, unit, precision=lax.Precision.HIGHEST)]
  transfers between devices with their start and end apart: 3 -> 0, of which waited for: 3 -> 0; matrix products, arithmetic and copies ran while one was open for 0% -> 0% of each run, Pallas kernels for 0% -> 0%
where the time goes in v1:
time: 90 us; the launch traced here: 89.8 us
  Pallas kernels  83.4 us (93%)
  local copies, waits for them, and re-layouts  5.04 us (6%)
  between operations  1.29 us (1%)
    pallas_call x1, Pallas kernels, local(): pl.pallas_call(functools.partial(kernel, n, m, local_rows * n * m), out_s...  83.4 us
    pallas_call x2, local copies, waits for them, and re-layouts, local(): pl.pallas_call(functools.partial(kernel, n, m, local_rows * n * m), out_s...  3.54 us

profile of v1, /device:TPU:0, one launch (start us, length us, event | category | flops | bytes accessed | tf_op | source)
XLA Modules:
  0.0 89.8 jit_solution(17917127241229471149)
XLA Ops:
  1.3 1.5 %copy.8.start = bf16[256,64]{1,0:T(8,128)(2,1)} copy(bf16[256,64]{0,1:T(8,128)(2,1)} %param.10) | data formatting | bytes 65536 | tf_op args[4]
  2.8 83.4 %spectral.1 = (f32[256,64]{1,0:T(8,128)}, f32[1024,64]{1,0:T(8,128)}) custom-call(bf16[16,128,128]{2,1,0:T(8,128)(2,1)} %tiles.1, s32[16]{0:T(128)} %rows_ref.1, s32[16]{0:T(128)} %columns_ref.1, s32[1]{0:T(128)S(6)} %copy.11.count_ref, bf16[256,64]{1,0:T(8,128)(2,1)} %copy.8.start, s32[1,1024]{1,0:T(1,128)} %bitcast.1), custom_call_target="tpu_custom_call" | custom-call | tf_op jit(solution)/shard_map/spectral/pallas_call | solution.py:269
  86.2 1.6 %copy.9 = f32[256,64]{0,1:T(8,128)} copy(f32[256,64]{1,0:T(8,128)} %get-tuple-element.2) | data formatting | bytes 131072 | tf_op jit(solution)/shard_map/spectral/pallas_call | solution.py:269
  87.8 1.9 %copy.10 = f32[1024,64]{0,1:T(8,128)} copy(f32[1024,64]{1,0:T(8,128)} %get-tuple-element.3) | data formatting | bytes 524288 | tf_op jit(solution)/shard_map/spectral/pallas_call | solution.py:269

commit v2 on v1

--- a/solution.py
+++ b/solution.py
@@ -79,15 +79,26 @@
     table = jnp.concatenate([gram, jnp.where(rows == lanes, 1.0, 0.0).astype(F32)], axis=1)
     parts = [table[8 * b : 8 * b + 8] for b in range(k // 8)]
     sub = lax.broadcasted_iota(jnp.int32, (8, 2 * k), 0)
-    for i in range(k):
+    for i in range(0, k, 2):
         b, r = divmod(i, 8)
-        row = parts[b][r : r + 1]
-        scaled = row / row[:, i : i + 1]
-        own = parts[b] - parts[b][:, i : i + 1] * scaled
-        if r < 7:
-            parts[b] = jnp.where(sub > r, own, parts[b])
+        own = parts[b]
+        top, low = own[r : r + 1], own[r + 1 : r + 2]
+        pivot, cross, corner = (
+            jnp.broadcast_to(v, (1, 2 * k))
+            for v in (top[:, i : i + 1], top[:, i + 1 : i + 2], low[:, i + 1 : i + 2])
+        )
+        over = 1.0 / pivot
+        ratio = cross * over
+        scaled_low = (low - ratio * top) / (corner - ratio * cross)
+        scaled_top = (top - cross * scaled_low) * over
+
+        def minus(part):
+            return part - part[:, i : i + 1] * scaled_top - part[:, i + 1 : i + 2] * scaled_low
+
+        fixed = jnp.where(sub == r + 1, own - ratio * top, own)
+        parts[b] = jnp.where(sub > r + 1, minus(own), fixed) if r < 6 else fixed
         for c in range(b + 1, k // 8):
-            parts[c] = parts[c] - parts[c][:, i : i + 1] * scaled
+            parts[c] = minus(parts[c])
     table = jnp.concatenate(parts, axis=0)
     diag = jnp.sum(jnp.where(rows == lanes, table[:, :k], 0.0), axis=1, keepdims=True)
     return table[:, k:] / jnp.sqrt(diag)
@@ -109,13 +120,14 @@
     unit_out, centres_out,
     matrix, basis0, basis1, images, gram_dev, gram_group,
     seed_out, seed_dev, seed_group, seed_all,
-    k_out, k_dev, k_group, k_all,
-    *sems,
+    *rest,
 ):
     me, g = lax.axis_index("dev"), lax.axis_index("group")
+    k_out, k_dev, k_group, k_all = (rest[2 * i : 2 * i + 2] for i in range(4))
+    sems = rest[8:]
     pairs = [(sems[2 * i], sems[2 * i + 1]) for i in range(len(sems) // 2)]
     slots, block = tiles.shape[0], tiles.shape[1]
-    local_rows, width = start.shape
+    width, local_rows = start.shape
     row_blocks = local_rows // block
     clusters = seeds.shape[1]
     part = clusters // n
@@ -128,15 +140,8 @@
                 barrier, inc=1, device_id={axis: lax.rem(index + 1 + i, size)}, device_id_type=MESH
             ),
         )
-    eye = jnp.where(
-        lax.broadcasted_iota(jnp.int32, (width, width), 0)
-        == lax.broadcasted_iota(jnp.int32, (width, width), 1),
-        1.0,
-        0.0,
-    ).astype(jnp.bfloat16)
-    start_t = lax.dot_general(eye, start[...], NT, preferred_element_type=F32)
     for r in range(row_blocks):
-        basis0[me * row_blocks + r] = start_t[:, r * block : (r + 1) * block].astype(jnp.bfloat16)
+        basis0[me * row_blocks + r] = start[:, r * block : (r + 1) * block]
     pl.semaphore_wait(barrier, n - 1 + m - 1)
 
     used = iter(pairs)
@@ -191,30 +196,60 @@
     image = apply(basis1)
     first = start_gram(image, 1)
 
-    def split(values, out, lo, hi):
-        for c in range(n):
-            out[c, lo:hi] = values[:, c * part : (c + 1) * part]
-
-    def join(ref):
-        return jnp.concatenate([ref[c] for c in range(n)], axis=1)
+    half = width // 2
+
+    def split(values, out, extra=None):
+        for h in range(2):
+            for c in range(n):
+                lanes = slice(c * part, (c + 1) * part)
+                out[h][c, :half] = values[h * half : (h + 1) * half, lanes]
+                if h == 0 and extra is not None:
+                    out[h][c, half:] = jnp.broadcast_to(extra[:, lanes], (8, part))
+
+    def join(refs):
+        return jnp.concatenate(
+            [jnp.concatenate([ref[c] for c in range(n)], axis=1) for ref in refs], axis=0
+        )
+
+    def start_dev(out, dev):
+        made = []
+        for h in range(2):
+            dev[h][me] = out[h][me]
+            made.append(
+                exchange("dev", lambda d, h=h: dev[h].at[d], lambda p, h=h: out[h].at[p])
+            )
+        return made
+
+    def start_group(made, dev, group):
+        after = []
+        for h in range(2):
+            made[h].wait_recv()
+            group[h][g] = fold(n, dev[h])
+            after.append(exchange("group", lambda d, h=h: group[h].at[d]))
+        return after
+
+    def start_all(made, group, every, finish):
+        after = []
+        for h in range(2):
+            made[h].wait_recv()
+            every[h][me] = finish(h, fold(m, group[h]))
+            after.append(exchange("dev", lambda d, h=h: every[h].at[d]))
+        return after
 
     first_row = (g * n + me) * local_rows
     chooser = jnp.where(
         lax.broadcasted_iota(jnp.int32, (local_rows, clusters), 0) == seeds[...] - first_row, 1.0, 0.0
     ).astype(F32)
-    split(mm(image, chooser), seed_out, 0, width)
-    seed_dev[me] = seed_out[me]
-    reduce_dev = exchange("dev", lambda d: seed_dev.at[d], lambda p: seed_out.at[p])
+    seed_out, seed_dev, seed_group, seed_all = (
+        [ref.at[h] for h in range(2)] for ref in (seed_out, seed_dev, seed_group, seed_all)
+    )
+    split(mm(image, chooser), seed_out)
+    made = start_dev(seed_out, seed_dev)
     second = end_gram(first, 1)
-    reduce_dev.wait_recv()
-    seed_group[g] = fold(n, seed_dev)
-    reduce_group = exchange("group", lambda d: seed_group.at[d])
+    made = start_group(made, seed_dev, seed_group)
     second.wait_recv()
-    packed = fold(m, gram_group.at[1])
-    reduce_group.wait_recv()
-    seed_all[me] = fold(m, seed_group)
-    gather = exchange("dev", lambda d: seed_all.at[d])
-    inverse = factor_inverse(unpack(packed))
+    inverse = factor_inverse(unpack(fold(m, gram_group.at[1])))
+    made = start_all(made, seed_group, seed_all, lambda h, total: total)
 
     def normalise(image_t):
         embedding = mm(inverse, image_t) * jnp.sqrt(F32(total_rows))
@@ -222,31 +257,31 @@
 
     unit_t = normalise(image)
     unit = unit_t.T
-    unit_out[...] = unit
+    unit_out[...] = unit_t
     unit_square = jnp.sum(unit * unit, axis=1, keepdims=True)
-    gather.wait_recv()
+    for gather in made:
+        gather.wait_recv()
     centres = normalise(join(seed_all))
     for turn in range(KSTEPS):
         dist = unit_square - 2.0 * mm(unit, centres) + jnp.sum(centres * centres, axis=0, keepdims=True)
         weights = jnp.exp(-SHARPNESS * dist)
         member = weights / jnp.sum(weights, axis=1, keepdims=True)
-        split(mm(unit_t, member), k_out.at[turn], 0, width)
-        mass = jnp.sum(member, axis=0, keepdims=True)
-        split(jnp.broadcast_to(mass, (8, clusters)), k_out.at[turn], width, width + 8)
-        k_dev[turn, me] = k_out[turn, me]
-        reduce_dev = exchange(
-            "dev", lambda d: k_dev.at[turn, d], lambda p: k_out.at[turn, p]
-        )
-        reduce_dev.wait_recv()
-        k_group[turn, g] = fold(n, k_dev.at[turn])
-        reduce_group = exchange("group", lambda d: k_group.at[turn, d])
-        reduce_group.wait_recv()
-        sums = fold(m, k_group.at[turn])
-        k_all[turn, me] = sums[:width] / sums[width : width + 1]
-        gather = exchange("dev", lambda d: k_all.at[turn, d])
-        gather.wait_recv()
-        centres = join(k_all.at[turn])
-    centres_out[...] = centres.T
+        out, dev, group, every = (
+            [ref.at[turn] for ref in refs] for refs in (k_out, k_dev, k_group, k_all)
+        )
+        split(mm(unit_t, member), out, jnp.sum(member, axis=0, keepdims=True))
+        made = start_group(start_dev(out, dev), dev, group)
+        mass = []
+
+        def finish(h, total):
+            if h == 0:
+                mass.append(total[half : half + 1])
+            return total[:half] / mass[0]
+
+        for gather in start_all(made, group, every, finish):
+            gather.wait_recv()
+        centres = join(every)
+    centres_out[...] = centres
     for made in pending:
         made.wait_send()
 
@@ -261,16 +296,16 @@
     vmem = pl.BlockSpec(memory_space=pltpu.VMEM)
     smem = pl.BlockSpec(memory_space=pltpu.SMEM)
     half = (width // 2, 2 * width)
-    axes = ["dev", "dev", "dev", "group", "dev", "dev", "group", "group", "dev"]
-    axes += ["dev", "group", "dev"] * KSTEPS
+    axes = ["dev", "dev", "dev", "group", "dev", "dev", "dev", "group", "group", "group", "dev", "dev"]
+    axes += ["dev", "dev", "group", "group", "dev", "dev"] * KSTEPS
     sems = []
     for axis in axes:
         sems += [pltpu.SemaphoreType.DMA((n if axis == "dev" else m,))] * 2
-    return pl.pallas_call(
+    unit, centres = pl.pallas_call(
         functools.partial(kernel, n, m, local_rows * n * m),
         out_shape=(
-            jax.ShapeDtypeStruct((local_rows, width), F32),
-            jax.ShapeDtypeStruct((clusters, width), F32),
+            jax.ShapeDtypeStruct((width, local_rows), F32),
+            jax.ShapeDtypeStruct((width, clusters), F32),
         ),
         in_specs=[vmem, smem, smem, smem, vmem, vmem],
         out_specs=(vmem, vmem),
@@ -281,21 +316,20 @@
             pltpu.VMEM((n, width, local_rows), F32),
             pltpu.VMEM((2, n, *half), F32),
             pltpu.VMEM((2, m, *half), F32),
-            pltpu.VMEM((n, width, part), F32),
-            pltpu.VMEM((n, width, part), F32),
-            pltpu.VMEM((m, width, part), F32),
-            pltpu.VMEM((n, width, part), F32),
-            pltpu.VMEM((KSTEPS, n, width + 8, part), F32),
-            pltpu.VMEM((KSTEPS, n, width + 8, part), F32),
-            pltpu.VMEM((KSTEPS, m, width + 8, part), F32),
-            pltpu.VMEM((KSTEPS, n, width, part), F32),
+            *[pltpu.VMEM((2, size, width // 2, part), F32) for size in (n, n, m, n)],
+            *[
+                pltpu.VMEM((KSTEPS, size, width // 2 + more, part), F32)
+                for size, extra in ((n, 8), (n, 8), (m, 8), (n, 0))
+                for more in (extra, 0)
+            ],
             *sems,
         ],
         compiler_params=pltpu.CompilerParams(
             collective_id=0, has_side_effects=True, vmem_limit_bytes=58 * 1024 * 1024
         ),
         name="spectral",
-    )(tile_values, tile_rows, tile_columns, tile_count, start_basis, seed_rows[None, :])
+    )(tile_values, tile_rows, tile_columns, tile_count, start_basis.T, seed_rows[None, :])
+    return unit.T, centres.T
 
 
 def solution(mesh):

time: 90 us -> 80 us (0.89)
  Pallas kernels: 83.4 us -> 75.4 us
  local copies, waits for them, and re-layouts: 5.04 us -> 3.14 us
    pallas_call x1, Pallas kernels: 83.4 us -> 75.4 us  [local(): pl.pallas_call(functools.partial(kernel, n, m, local_rows * n * m), out_s...]
    pallas_call x2 -> x0, local copies, waits for them, and re-layouts: 3.54 us -> none  [local(): pl.pallas_call(functools.partial(kernel, n, m, local_rows * n * m), out_s...]
    unnamed x1 -> x2, local copies, waits for them, and re-layouts: 1.49 us -> 3.14 us
where the time goes in v2:
time: 80 us; the launch traced here: 79.8 us
  Pallas kernels  75.4 us (94%)
  local copies, waits for them, and re-layouts  3.14 us (4%)
  between operations  1.29 us (2%)
    pallas_call x1, Pallas kernels, local(): pl.pallas_call(functools.partial(kernel, n, m, local_rows * n * m), out_s...  75.4 us
    unnamed x2, local copies, waits for them, and re-layouts  3.14 us

profile of v2, /device:TPU:0, one launch (start us, length us, event | category | flops | bytes accessed | tf_op | source)
XLA Modules:
  0.0 79.8 jit_solution(3612158261734735701)
XLA Ops:
  1.3 75.4 %spectral.1 = (f32[64,256]{1,0:T(8,128)}, f32[64,1024]{1,0:T(8,128)}) custom-call(bf16[16,128,128]{2,1,0:T(8,128)(2,1)} %tiles.1, s32[16]{0:T(128)} %rows_ref.1, s32[16]{0:T(128)} %columns_ref.1, s32[1]{0:T(128)S(6)} %copy.10.count_ref, bf16[64,256]{1,0:T(8,128)(2,1)} %bitcast.6, s32[1,1024]{1,0:T(1,128)} %bitcast.7), custom_call_target="tpu_custom_call" | custom-call | tf_op jit(solution)/shard_map/spectral/pallas_call | solution.py:304
  76.7 1.5 %copy.11 = f32[256,64]{0,1:T(8,128)} copy(f32[256,64]{0,1:T(8,128)} %bitcast.5) | data formatting | bytes 131072
  78.1 1.7 %copy.12 = f32[1024,64]{0,1:T(8,128)} copy(f32[1024,64]{0,1:T(8,128)} %bitcast.4) | data formatting | bytes 524288

commit v3 on v2

--- a/solution.py
+++ b/solution.py
@@ -9,6 +9,7 @@
 
 KSTEPS = 2
 SHARPNESS = 4.0
+MASS_ROWS = 16
 MESH = pl.DeviceIdType.MESH
 F32 = jnp.float32
 HIGHEST = lax.Precision.HIGHEST
@@ -20,6 +21,15 @@
     return lax.dot_general(a, b, dims, precision=HIGHEST, preferred_element_type=F32)
 
 
+def high_low(x):
+    high = x.astype(jnp.bfloat16)
+    return high, (x - high.astype(F32)).astype(jnp.bfloat16)
+
+
+def dot16(a, b):
+    return lax.dot_general(a, b, NN, preferred_element_type=F32)
+
+
 def loop(n, body):
     if n <= 8:
         for i in range(n):
@@ -34,12 +44,12 @@
 
 
 def fold(n, ref):
+    total = ref[0].astype(F32)
     if n <= 8:
-        total = ref[0]
         for i in range(1, n):
-            total = total + ref[i]
+            total = total + ref[i].astype(F32)
         return total
-    return lax.fori_loop(1, n, lambda i, total: total + ref[i], ref[0])
+    return lax.fori_loop(1, n, lambda i, total: total + ref[i].astype(F32), total)
 
 
 class Exchange:
@@ -202,9 +212,11 @@
         for h in range(2):
             for c in range(n):
                 lanes = slice(c * part, (c + 1) * part)
-                out[h][c, :half] = values[h * half : (h + 1) * half, lanes]
+                out[h][c, :half] = values[h * half : (h + 1) * half, lanes].astype(out[h].dtype)
                 if h == 0 and extra is not None:
-                    out[h][c, half:] = jnp.broadcast_to(extra[:, lanes], (8, part))
+                    out[h][c, half:] = jnp.broadcast_to(
+                        extra[:, lanes], (MASS_ROWS, part)
+                    ).astype(out[h].dtype)
 
     def join(refs):
         return jnp.concatenate(
@@ -224,7 +236,8 @@
         after = []
         for h in range(2):
             made[h].wait_recv()
-            group[h][g] = fold(n, dev[h])
+            total = fold(n, dev[h])
+            group[h][g] = total[: group[h].shape[1]]
             after.append(exchange("group", lambda d, h=h: group[h].at[d]))
         return after
 
@@ -239,11 +252,14 @@
     first_row = (g * n + me) * local_rows
     chooser = jnp.where(
         lax.broadcasted_iota(jnp.int32, (local_rows, clusters), 0) == seeds[...] - first_row, 1.0, 0.0
-    ).astype(F32)
+    ).astype(jnp.bfloat16)
+    high = image.astype(jnp.bfloat16)
+    rest_of = image - high.astype(F32)
+    pieces = dot16(jnp.concatenate([high, *high_low(rest_of)], axis=0), chooser)
     seed_out, seed_dev, seed_group, seed_all = (
         [ref.at[h] for h in range(2)] for ref in (seed_out, seed_dev, seed_group, seed_all)
     )
-    split(mm(image, chooser), seed_out)
+    split(pieces[:width] + pieces[width : 2 * width] + pieces[2 * width :], seed_out)
     made = start_dev(seed_out, seed_dev)
     second = end_gram(first, 1)
     made = start_group(made, seed_dev, seed_group)
@@ -256,20 +272,27 @@
         return embedding / jnp.sqrt(jnp.sum(embedding * embedding, axis=0, keepdims=True) + 1e-06)
 
     unit_t = normalise(image)
+    unit_out[...] = unit_t
     unit = unit_t.T
-    unit_out[...] = unit_t
     unit_square = jnp.sum(unit * unit, axis=1, keepdims=True)
+    unit_high, unit_low = high_low(unit_t)
+    left = jnp.concatenate([unit_high, unit_low, unit_high], axis=0).astype(F32).T.astype(jnp.bfloat16)
+    unit_pair = jnp.concatenate([unit_high, unit_low], axis=0)
     for gather in made:
         gather.wait_recv()
     centres = normalise(join(seed_all))
     for turn in range(KSTEPS):
-        dist = unit_square - 2.0 * mm(unit, centres) + jnp.sum(centres * centres, axis=0, keepdims=True)
+        high, low = high_low(centres)
+        inner = dot16(left, jnp.concatenate([high, high, low], axis=0))
+        dist = unit_square - 2.0 * inner + jnp.sum(centres * centres, axis=0, keepdims=True)
         weights = jnp.exp(-SHARPNESS * dist)
         member = weights / jnp.sum(weights, axis=1, keepdims=True)
         out, dev, group, every = (
             [ref.at[turn] for ref in refs] for refs in (k_out, k_dev, k_group, k_all)
         )
-        split(mm(unit_t, member), out, jnp.sum(member, axis=0, keepdims=True))
+        high, low = high_low(member)
+        pair = dot16(unit_pair, high)
+        split(pair[:width] + pair[width:] + dot16(unit_high, low), out, jnp.sum(member, axis=0, keepdims=True))
         made = start_group(start_dev(out, dev), dev, group)
         mass = []
 
@@ -318,8 +341,13 @@
             pltpu.VMEM((2, m, *half), F32),
             *[pltpu.VMEM((2, size, width // 2, part), F32) for size in (n, n, m, n)],
             *[
-                pltpu.VMEM((KSTEPS, size, width // 2 + more, part), F32)
-                for size, extra in ((n, 8), (n, 8), (m, 8), (n, 0))
+                pltpu.VMEM((KSTEPS, size, width // 2 + more, part), kind)
+                for size, extra, kind in (
+                    (n, MASS_ROWS, jnp.bfloat16),
+                    (n, MASS_ROWS, jnp.bfloat16),
+                    (m, 8, F32),
+                    (n, 0, F32),
+                )
                 for more in (extra, 0)
             ],
             *sems,

time: 80 us -> 75.7 us (0.946)
  Pallas kernels: 75.4 us -> 71 us
    pallas_call x1, Pallas kernels: 75.4 us -> 71 us  [local(): pl.pallas_call(functools.partial(kernel, n, m, local_rows * n * m), out_s...]
where the time goes in v3:
time: 75.7 us; the launch traced here: 75.5 us
  Pallas kernels  71 us (94%)
  local copies, waits for them, and re-layouts  3.14 us (4%)
  between operations  1.29 us (2%)
    pallas_call x1, Pallas kernels, local(): pl.pallas_call(functools.partial(kernel, n, m, local_rows * n * m), out_s...  71 us
    unnamed x2, local copies, waits for them, and re-layouts  3.14 us

profile of v3, /device:TPU:0, one launch (start us, length us, event | category | flops | bytes accessed | tf_op | source)
XLA Modules:
  0.0 75.5 jit_solution(6392650701562195612)
XLA Ops:
  1.3 71.0 %spectral.1 = (f32[64,256]{1,0:T(8,128)}, f32[64,1024]{1,0:T(8,128)}) custom-call(bf16[16,128,128]{2,1,0:T(8,128)(2,1)} %tiles.1, s32[16]{0:T(128)} %rows_ref.1, s32[16]{0:T(128)} %columns_ref.1, s32[1]{0:T(128)S(6)} %copy.10.count_ref, bf16[64,256]{1,0:T(8,128)(2,1)} %bitcast.6, s32[1,1024]{1,0:T(1,128)} %bitcast.7), custom_call_target="tpu_custom_call" | custom-call | tf_op jit(solution)/shard_map/spectral/pallas_call | solution.py:327
  72.3 1.5 %copy.11 = f32[256,64]{0,1:T(8,128)} copy(f32[256,64]{0,1:T(8,128)} %bitcast.5) | data formatting | bytes 131072
  73.8 1.7 %copy.12 = f32[1024,64]{0,1:T(8,128)} copy(f32[1024,64]{0,1:T(8,128)} %bitcast.4) | data formatting | bytes 524288

commit v4 on v3

--- a/solution.py
+++ b/solution.py
@@ -133,8 +133,8 @@
     *rest,
 ):
     me, g = lax.axis_index("dev"), lax.axis_index("group")
-    k_out, k_dev, k_group, k_all = (rest[2 * i : 2 * i + 2] for i in range(4))
-    sems = rest[8:]
+    k_out, k_dev, k_group, k_all, k_early = (rest[2 * i : 2 * i + 2] for i in range(5))
+    sems = rest[10:]
     pairs = [(sems[2 * i], sems[2 * i + 1]) for i in range(len(sems) // 2)]
     slots, block = tiles.shape[0], tiles.shape[1]
     width, local_rows = start.shape
@@ -237,7 +237,7 @@
         for h in range(2):
             made[h].wait_recv()
             total = fold(n, dev[h])
-            group[h][g] = total[: group[h].shape[1]]
+            group[h][g] = total[: group[h].shape[1]].astype(group[h].dtype)
             after.append(exchange("group", lambda d, h=h: group[h].at[d]))
         return after
 
@@ -288,7 +288,8 @@
         weights = jnp.exp(-SHARPNESS * dist)
         member = weights / jnp.sum(weights, axis=1, keepdims=True)
         out, dev, group, every = (
-            [ref.at[turn] for ref in refs] for refs in (k_out, k_dev, k_group, k_all)
+            [ref.at[turn] for ref in refs]
+            for refs in (k_out, k_dev, k_group if turn + 1 == KSTEPS else k_early, k_all)
         )
         high, low = high_low(member)
         pair = dot16(unit_pair, high)
@@ -347,6 +348,7 @@
                     (n, MASS_ROWS, jnp.bfloat16),
                     (m, 8, F32),
                     (n, 0, F32),
+                    (m, MASS_ROWS, jnp.bfloat16),
                 )
                 for more in (extra, 0)
             ],

time: 75.7 us -> 74.8 us (0.988)
  Pallas kernels: 71 us -> 70.2 us
    pallas_call x1, Pallas kernels: 71 us -> 70.2 us  [local(): pl.pallas_call(functools.partial(kernel, n, m, local_rows * n * m), out_s...]
where the time goes in v4:
time: 74.8 us; the launch traced here: 74.6 us
  Pallas kernels  70.2 us (94%)
  local copies, waits for them, and re-layouts  3.14 us (4%)
  between operations  1.29 us (2%)
    pallas_call x1, Pallas kernels, local(): pl.pallas_call(functools.partial(kernel, n, m, local_rows * n * m), out_s...  70.2 us
    unnamed x2, local copies, waits for them, and re-layouts  3.14 us

profile of v4, /device:TPU:0, one launch (start us, length us, event | category | flops | bytes accessed | tf_op | source)
XLA Modules:
  0.0 74.6 jit_solution(17979005819687735423)
XLA Ops:
  1.3 70.2 %spectral.1 = (f32[64,256]{1,0:T(8,128)}, f32[64,1024]{1,0:T(8,128)}) custom-call(bf16[16,128,128]{2,1,0:T(8,128)(2,1)} %tiles.1, s32[16]{0:T(128)} %rows_ref.1, s32[16]{0:T(128)} %columns_ref.1, s32[1]{0:T(128)S(6)} %copy.10.count_ref, bf16[64,256]{1,0:T(8,128)(2,1)} %bitcast.6, s32[1,1024]{1,0:T(1,128)} %bitcast.7), custom_call_target="tpu_custom_call" | custom-call | tf_op jit(solution)/shard_map/spectral/pallas_call | solution.py:328
  71.5 1.5 %copy.11 = f32[256,64]{0,1:T(8,128)} copy(f32[256,64]{0,1:T(8,128)} %bitcast.5) | data formatting | bytes 131072
  73.0 1.7 %copy.12 = f32[1024,64]{0,1:T(8,128)} copy(f32[1024,64]{0,1:T(8,128)} %bitcast.4) | data formatting | bytes 524288
